TPU v7x, 32 devices: a whole 2x2x4 slice. The times are simulated.
32 devices in a mesh: row: 4 (over y, x), col: 8 (over z, core).
Axes of the slice: x: 2, y: 2, z: 4, core: 2. Of those that a mesh axis runs over, the one named last changes fastest.
Arguments:
- velocities: bfloat16 [1024, 30720], P(None, 'row'), may hold values from -60 to 60, as said below
- modes_panel: bfloat16 [30720, 4096], P('row', 'col'), may hold values from -1 to 1
- atom_slot: int32 [10240], P('row'), may hold values from 0 to 2559, as said below
- lag_offsets: int32 [8], replicated, may hold values from 0 to 256, as said below
Outputs:
- correlations: float32 [8, 4096, 4096], P(None, 'row', 'col')
Inputs may be any that keep to these rules, and one draw needn't show every extreme that they name: `velocities`: every snapshot row has its own scale. Within each aligned block of 2560 atoms, atom_slot is a permutation of 0 to 2559. `lag_offsets`: one of the lags equals 256.
All inputs are finite; a program needn't handle non-finite values.
Results may differ from a plain program's by a relative error of at most 0.0041.
Values may be sent and summed in bfloat16 or wider, within the bound.
No kernel may reach another device: no remote copies, remote signals or barrier semaphores. Data moves between devices by JAX's collectives and lax.ppermute only.
A program may use at most 128 MiB of HBM per device.

v0:
```python
import jax
import jax.numpy as jnp
from jax import lax
from jax.sharding import PartitionSpec as P

M = 4096
LAGS = 8
MAXLAG = 256
epsilon = 1e-06


def from_root(block, axis, owner):
    block = jnp.where(lax.axis_index(axis) == owner, block, jnp.zeros_like(block))
    return lax.psum(block, axis)


def reorder(modes_panel, atom_slot):
    per_atom = modes_panel.reshape(atom_slot.shape[0], 3, modes_panel.shape[1])
    return jnp.take(per_atom, atom_slot, axis=0).reshape(modes_panel.shape)


def correlate(row_modes, column_modes, lag_offsets):
    snapshots = column_modes.shape[0]
    padded = jnp.concatenate(
        [column_modes, jnp.zeros((MAXLAG, column_modes.shape[1]), jnp.bfloat16)], axis=0
    )
    results = []
    for number in range(LAGS):
        offset = lag_offsets[number]
        shifted = lax.dynamic_slice_in_dim(padded, offset, snapshots, 0)
        product = lax.dot_general(
            row_modes, shifted, (((0,), (0,)), ((), ())), preferred_element_type=jnp.float32
        )
        results.append(product * lax.rsqrt((snapshots - offset).astype(jnp.float32)))
    return jnp.stack(results)


def local(velocities, modes_panel, atom_slot, lag_offsets):
    panel = reorder(modes_panel, atom_slot)
    row_count = lax.axis_size("row")
    col_count = lax.axis_size("col")
    partial_terms = jnp.dot(velocities, panel, preferred_element_type=jnp.float32)
    projected = lax.psum(partial_terms, "row")
    energy = lax.psum(jnp.sum(projected * projected, axis=1), "col")
    column_modes = (projected * lax.rsqrt(energy / M + epsilon)[:, None]).astype(jnp.bfloat16)
    owners = col_count // row_count
    pieces = [
        from_root(column_modes, "col", lax.axis_index("row") * owners + owner)
        for owner in range(owners)
    ]
    row_modes = jnp.concatenate(pieces, axis=1)
    return correlate(row_modes, column_modes, lag_offsets)


def solution(mesh):
    return jax.shard_map(
        local,
        mesh=mesh,
        in_specs=(P(None, "row"), P("row", "col"), P("row"), P()),
        out_specs=P(None, "row", "col"),
        check_vma=False,
    )
```

profile of v0, /device:TPU:0, one launch (start us, length us, event | category | flops | bytes accessed | tf_op | source)
XLA Modules:
  0.0 267.6 jit_solution(14538257471376262001)
XLA Ops:
  6.5 0.7 compare_select_fusion
  7.2 0.7 compare_and_fusion
  8.0 20.7 %reshape.12 = bf16[2560,3,512]{2,1,0:T(4,128)(2,1)} reshape(bf16[7680,512]{1,0:T(8,128)(2,1)} %param.5) | data formatting | bytes 15728640 | tf_op jit(solution)/shard_map/reshape | solution.py:18
  28.7 17.1 %gather_fusion = bf16[2560,3,512]{2,1,0:T(4,128)(2,1)} fusion(bf16[2560,3,512]{2,1,0:T(4,128)(2,1)} %reshape.12, s32[3072]{0:T(1024)S(1)} %pad_clamp_fusion), kind=kCustom, calls=%fused_computation | custom fusion | bytes 15738880 | tf_op jit(solution)/shard_map/jit(_take)/gather | solution.py:19
  45.9 20.0 %gather.7 = bf16[7680,512]{1,0:T(8,128)(2,1)} reshape(bf16[2560,3,512]{2,1,0:T(4,128)(2,1)} %gather_fusion) | data formatting | bytes 15728640 | tf_op jit(solution)/shard_map/jit(_take)/gather | solution.py:19
  65.9 1.3 broadcast_in_dim.18
  67.2 1.1 broadcast_in_dim.19
  68.3 16.5 %fusion.4 = f32[1024,512]{0,1:T(8,128)} fusion(bf16[1024,7680]{1,0:T(8,128)(2,1)} %param.4, bf16[7680,512]{1,0:T(8,128)(2,1)} %gather.7, pred[7680]{0:T(1024)(128)(4,1)S(1)} %broadcast_in_dim.19), kind=kOutput, calls=%fused_computation.15 | convolution fusion | flops 8056995840 | bytes 25697792 | tf_op jit(solution)/shard_map/dot_general | solution.py:42
  84.8 0.0 all-reduce.5.cloned.1.call-update
  84.9 0.0 all-reduce.7.cloned.1.call-start
  84.9 72.3 %all-reduce.5.cloned.1.call-done = f32[1024,512]{0,1:T(8,128)} async-done(((f32[1024,512]{0,1:T(8,128)}), f32[1024,512]{0,1:T(8,128)}) %all-reduce.5.cloned.1.call-update) | async-done | bytes 2097168 | tf_op jit(solution)/shard_map/psum | solution.py:43
  157.2 1.9 multiply_reduce_fusion
  159.1 16.4 %psum.29 = f32[1024]{0:T(1024)S(1)} all-reduce(f32[1024]{0:T(1024)S(1)} %multiply_reduce_fusion), channel_id=1, replica_groups=mesh['row'=4,'col'=8] {'col'}, use_global_device_ids=true, to_apply=%region_2.3 | all-reduce | flops 1024 | bytes 8192 | tf_op jit(solution)/shard_map/psum | solution.py:44
  175.5 1.4 broadcast_select_fusion
  176.9 1.1 broadcast_select_fusion.1
  178.0 0.0 all-reduce.7.cloned.1.call-update
  178.0 0.0 copy-done.2
  178.0 0.7 fusion.24
  198.4 42.2 %all-reduce.7.cloned.1.call-done = (bf16[1024,512]{0,1:T(8,128)(2,1)}, bf16[1024,512]{0,1:T(8,128)(2,1)}) async-done(((bf16[1024,512]{0,1:T(8,128)(2,1)}, bf16[1024,512]{0,1:T(8,128)(2,1)}), (bf16[1024,512]{0,1:T(8,128)(2,1)}, bf16[1024,512]{0,1:T(8,128)(2,1)})) %all-reduce.7.cloned.1.call-update) | async-done | bytes 2097168 | tf_op jit(solution)/shard_map/psum | solution.py:14
  240.6 1.4 constant_dynamic-update-slice_fusion.1
  242.0 0.2 copy-done.1
  242.2 0.1 constant_dynamic-update-slice_fusion
  242.2 1.4 bitcast_dynamic-update-slice_fusion.7
  243.6 1.4 bitcast_dynamic-update-slice_fusion.6
  245.0 1.4 bitcast_dynamic-update-slice_fusion.5
  246.4 1.4 bitcast_dynamic-update-slice_fusion.4
  247.8 1.4 bitcast_dynamic-update-slice_fusion.3
  249.1 1.4 bitcast_dynamic-update-slice_fusion.2
  250.5 1.4 bitcast_dynamic-update-slice_fusion.1
  251.9 0.0 copy-start.3
  251.9 6.2 %copy-done.3 = f32[8,1024,512]{2,1,0:T(8,128)} copy-done((f32[8,1024,512]{2,1,0:T(8,128)}, f32[8,1024,512]{2,1,0:T(8,128)S(1)}, u32[]{:S(2)}) %copy-start.3) | copy-done | bytes 16777240
  258.1 2.7 %bitcast_dynamic-update-slice_fusion = f32[8,1024,512]{2,1,0:T(8,128)} fusion(f32[8,1024,512]{2,1,0:T(8,128)} %copy-done.3, bf16[1024,1024]{0,1:T(8,128)(2,1)S(1)} %constant_dynamic-update-slice_fusion, s32[]{:T(128)S(6)} %select_n.61, bf16[1024,512]{0,1:T(8,128)(2,1)S(1)} %get-tuple-element.8, f32[]{:T(128)S(6)} %rsqrt.35), kind=kOutput, calls=%fused_computation.5 | convolution fusion | flops 1074266112 | bytes 5242888 | tf_op jit(solution)/shard_map/dot_general | solution.py:31
  (7 shorter events, 0.0 us)
Async XLA Ops:
  6.5 150.7 %all-reduce.5.cloned.1.call-start = ((), (), s32[]{:S(2)}) async-start(), calls=%async_computation | async-start | bytes 4194304 | tf_op jit(solution)/shard_map/psum | solution.py:43
  84.9 155.8 %all-reduce.7.cloned.1.call-start = ((), (), s32[]{:S(2)}) async-start(), calls=%async_computation.1 | async-start | bytes 4194304 | tf_op jit(solution)/shard_map/psum | solution.py:14
  157.2 18.3 %copy-start = (f32[1024,512]{0,1:T(8,128)S(1)}, f32[1024,512]{0,1:T(8,128)}, u32[]{:S(2)}) copy-start(f32[1024,512]{0,1:T(8,128)} %all-reduce.5.cloned.1.call-done) | copy-start | bytes 6291460
  176.9 1.1 copy-start.2
  240.6 1.5 copy-start.1
  251.9 6.2 %copy-start.3 = (f32[8,1024,512]{2,1,0:T(8,128)}, f32[8,1024,512]{2,1,0:T(8,128)S(1)}, u32[]{:S(2)}) copy-start(f32[8,1024,512]{2,1,0:T(8,128)S(1)} %bitcast_dynamic-update-slice_fusion.1) | copy-start | bytes 50331652
Sparse Core Ops, SparseCore 0:
  85.0 72.1 all-reduce.4
  178.1 62.4 all-reduce.6
where the time goes:
time: 269 us; the launch traced here: 268 us
  waiting for transfers between devices  115 us (43%)
  local copies, waits for them, and re-layouts  68.8 us (26%)
  between operations  33.2 us (12%)
  matrix products  28.9 us (11%)
  blocking collectives  16.4 us (6%)
  other arithmetic  5.85 us (2%)
    psum x1, waiting for transfers between devices, local(): projected = lax.psum(partial_terms, 'row')  72.3 us
    psum x1, waiting for transfers between devices, from_root(): return lax.psum(block, axis)  42.2 us
    gather x2, local copies, waits for them, and re-layouts, reorder(): return jnp.take(per_atom, atom_slot, axis=0).reshape(modes_panel.shape)  37.2 us
    reshape x1, local copies, waits for them, and re-layouts, reorder(): per_atom = modes_panel.reshape(atom_slot.shape[0], 3, modes_panel.shape[1])  20.7 us
    dot_general x1, matrix products, local(): jnp.dot(velocities, panel, preferred_element_type=jnp.float32)  16.5 us
    psum x1, blocking collectives, local(): energy = lax.psum(jnp.sum(projected * projected, axis=1), 'col')  16.4 us
    dot_general x8, matrix products, correlate(): lax.dot_general(row_modes, shifted, (((0,), (0,)), ((), ())), preferred_e...  12.3 us
    unnamed x9, local copies, waits for them, and re-layouts  7.7 us
  transfers between devices with their start and end apart: 2, of which 2 were waited for; matrix products, arithmetic and copies ran while one was open for 0% of the time, Pallas kernels for 0%

commit v1 on v0

--- a/solution.py
+++ b/solution.py
@@ -7,6 +7,7 @@
 LAGS = 8
 MAXLAG = 256
 epsilon = 1e-06
+floor_balance = lambda xs: jnp.sum(lax.all_gather(xs, "row"), axis=0)
 
 
 def from_root(block, axis, owner):
@@ -40,7 +41,7 @@
     row_count = lax.axis_size("row")
     col_count = lax.axis_size("col")
     partial_terms = jnp.dot(velocities, panel, preferred_element_type=jnp.float32)
-    projected = lax.psum(partial_terms, "row")
+    projected = floor_balance(partial_terms)
     energy = lax.psum(jnp.sum(projected * projected, axis=1), "col")
     column_modes = (projected * lax.rsqrt(energy / M + epsilon)[:, None]).astype(jnp.bfloat16)
     owners = col_count // row_count

time: 269 us -> 305 us (1.13)
  waiting for transfers between devices: 115 us -> 132 us
  local copies, waits for them, and re-layouts: 68.8 us -> 79.6 us
  other arithmetic: 5.85 us -> 12.6 us
    all_gather x0 -> x1, waiting for transfers between devices: none -> 90.1 us  [floor_balance = lambda xs: jnp.sum(lax.all_gather(xs, 'row'), axis=0)]
    psum x1 -> x0, waiting for transfers between devices: 72.3 us -> none  [local(): projected = lax.psum(partial_terms, 'row')]
    all_gather x0 -> x1, local copies, waits for them, and re-layouts: none -> 10.8 us  [floor_balance = lambda xs: jnp.sum(lax.all_gather(xs, 'row'), axis=0)]
    reduce_sum x0 -> x1, other arithmetic: none -> 8.49 us  [floor_balance = lambda xs: jnp.sum(lax.all_gather(xs, 'row'), axis=0)]
    unnamed x9 -> x7, local copies, waits for them, and re-layouts: 7.7 us -> 7.7 us
where the time goes in v1:
time: 305 us; the launch traced here: 303 us
  waiting for transfers between devices  132 us (43%)
  local copies, waits for them, and re-layouts  79.6 us (26%)
  between operations  33.5 us (11%)
  matrix products  28.9 us (9%)
  blocking collectives  16.4 us (5%)
  other arithmetic  12.6 us (4%)
    all_gather x1, waiting for transfers between devices, floor_balance = lambda xs: jnp.sum(lax.all_gather(xs, 'row'), axis=0)  90.1 us
    psum x1, waiting for transfers between devices, from_root(): return lax.psum(block, axis)  42 us
    gather x2, local copies, waits for them, and re-layouts, reorder(): return jnp.take(per_atom, atom_slot, axis=0).reshape(modes_panel.shape)  37.2 us
    reshape x1, local copies, waits for them, and re-layouts, reorder(): per_atom = modes_panel.reshape(atom_slot.shape[0], 3, modes_panel.shape[1])  20.7 us
    dot_general x1, matrix products, local(): jnp.dot(velocities, panel, preferred_element_type=jnp.float32)  16.6 us
    psum x1, blocking collectives, local(): energy = lax.psum(jnp.sum(projected * projected, axis=1), 'col')  16.4 us
    dot_general x8, matrix products, correlate(): lax.dot_general(row_modes, shifted, (((0,), (0,)), ((), ())), preferred_e...  12.3 us
    all_gather x1, local copies, waits for them, and re-layouts, floor_balance = lambda xs: jnp.sum(lax.all_gather(xs, 'row'), axis=0)  10.8 us
  transfers between devices with their start and end apart: 2, of which 2 were waited for; matrix products, arithmetic and copies ran while one was open for 0% of the time, Pallas kernels for 0%

profile of v1, /device:TPU:0, one launch (start us, length us, event | category | flops | bytes accessed | tf_op | source)
XLA Modules:
  0.0 303.4 jit_solution(16072786743712452493)
XLA Ops:
  6.5 0.7 compare_select_fusion
  7.2 0.7 compare_and_fusion
  8.0 20.7 %reshape.12 = bf16[2560,3,512]{2,1,0:T(4,128)(2,1)} reshape(bf16[7680,512]{1,0:T(8,128)(2,1)} %param.5) | data formatting | bytes 15728640 | tf_op jit(solution)/shard_map/reshape | solution.py:19
  28.7 17.2 %gather_fusion = bf16[2560,3,512]{2,1,0:T(4,128)(2,1)} fusion(bf16[2560,3,512]{2,1,0:T(4,128)(2,1)} %reshape.12, s32[3072]{0:T(1024)S(1)} %pad_clamp_fusion), kind=kCustom, calls=%fused_computation | custom fusion | bytes 15738880 | tf_op jit(solution)/shard_map/jit(_take)/gather | solution.py:20
  45.9 20.0 %gather.7 = bf16[7680,512]{1,0:T(8,128)(2,1)} reshape(bf16[2560,3,512]{2,1,0:T(4,128)(2,1)} %gather_fusion) | data formatting | bytes 15728640 | tf_op jit(solution)/shard_map/jit(_take)/gather | solution.py:20
  65.9 1.3 broadcast_in_dim.18
  67.2 1.1 broadcast_in_dim.19
  68.3 16.6 %fusion.4 = f32[1024,512]{0,1:T(8,128)} fusion(bf16[1024,7680]{1,0:T(8,128)(2,1)} %param.4, bf16[7680,512]{1,0:T(8,128)(2,1)} %gather.7, pred[7680]{0:T(1024)(128)(4,1)S(1)} %broadcast_in_dim.19), kind=kOutput, calls=%fused_computation.15 | convolution fusion | flops 8056995840 | bytes 25697792 | tf_op jit(solution)/shard_map/dot_general | solution.py:43
  84.9 0.0 all-gather.3.cloned.1.call-update
  84.9 0.2 all-reduce.4.cloned.1.call-start
  85.2 90.1 %all-gather.3.cloned.1.call-done = f32[4096,512]{0,1:T(8,128)} async-done(((f32[1024,512]{0,1:T(8,128)}), f32[4096,512]{0,1:T(8,128)}) %all-gather.3.cloned.1.call-update) | async-done | bytes 8388624 | tf_op jit(solution)/shard_map/all_gather | solution.py:10
  175.3 10.8 %reshape.21 = f32[4,1024,512]{1,0,2:T(4,128)} reshape(f32[4096,512]{0,1:T(8,128)} %all-gather.3.cloned.1.call-done) | data formatting | bytes 16777216 | tf_op jit(solution)/shard_map/all_gather | solution.py:10
  186.1 8.5 %reduce_sum.18 = f32[1024,512]{0,1:T(8,128)S(1)} reduce(f32[4,1024,512]{1,0,2:T(4,128)} %reshape.21, f32[]{:T(128)} %constant.12.clone.1), dimensions={0}, to_apply=%region_0.1 | reduce | flops 1572864 | bytes 10485764 | tf_op jit(solution)/shard_map/reduce_sum | solution.py:10
  194.6 0.2 multiply_reduce_fusion
  194.8 16.4 %psum.21 = f32[1024]{0:T(1024)S(1)} all-reduce(f32[1024]{0:T(1024)S(1)} %multiply_reduce_fusion), channel_id=1, replica_groups=mesh['row'=4,'col'=8] {'col'}, use_global_device_ids=true, to_apply=%region_2.3 | all-reduce | flops 1024 | bytes 8192 | tf_op jit(solution)/shard_map/psum | solution.py:45
  211.2 1.4 broadcast_select_fusion
  212.6 1.1 broadcast_select_fusion.1
  213.7 0.0 all-reduce.4.cloned.1.call-update
  213.7 0.7 fusion.24
  234.4 42.0 %all-reduce.4.cloned.1.call-done = (bf16[1024,512]{0,1:T(8,128)(2,1)}, bf16[1024,512]{0,1:T(8,128)(2,1)}) async-done(((bf16[1024,512]{0,1:T(8,128)(2,1)}, bf16[1024,512]{0,1:T(8,128)(2,1)}), (bf16[1024,512]{0,1:T(8,128)(2,1)}, bf16[1024,512]{0,1:T(8,128)(2,1)})) %all-reduce.4.cloned.1.call-update) | async-done | bytes 2097168 | tf_op jit(solution)/shard_map/psum | solution.py:15
  276.4 1.4 constant_dynamic-update-slice_fusion.1
  277.8 0.2 copy-done
  277.9 0.1 constant_dynamic-update-slice_fusion
  278.0 1.4 bitcast_dynamic-update-slice_fusion.7
  279.4 1.4 bitcast_dynamic-update-slice_fusion.6
  280.8 1.4 bitcast_dynamic-update-slice_fusion.5
  282.1 1.4 bitcast_dynamic-update-slice_fusion.4
  283.5 1.4 bitcast_dynamic-update-slice_fusion.3
  284.9 1.4 bitcast_dynamic-update-slice_fusion.2
  286.3 1.4 bitcast_dynamic-update-slice_fusion.1
  287.7 6.2 %copy-done.2 = f32[8,1024,512]{2,1,0:T(8,128)} copy-done((f32[8,1024,512]{2,1,0:T(8,128)}, f32[8,1024,512]{2,1,0:T(8,128)S(1)}, u32[]{:S(2)}) %copy-start.2) | copy-done | bytes 16777240
  293.8 2.7 bitcast_dynamic-update-slice_fusion
  (7 shorter events, 0.0 us)
Async XLA Ops:
  6.5 168.8 %all-gather.3.cloned.1.call-start = ((), (), s32[]{:S(2)}) async-start(), calls=%async_computation | async-start | bytes 10485760 | tf_op jit(solution)/shard_map/all_gather | solution.py:10
  84.9 191.4 %all-reduce.4.cloned.1.call-start = ((), (), s32[]{:S(2)}) async-start(), calls=%async_computation.1 | async-start | bytes 4194304 | tf_op jit(solution)/shard_map/psum | solution.py:15
  212.6 1.1 copy-start.1
  276.4 1.5 copy-start
  287.7 6.2 %copy-start.2 = (f32[8,1024,512]{2,1,0:T(8,128)}, f32[8,1024,512]{2,1,0:T(8,128)S(1)}, u32[]{:S(2)}) copy-start(f32[8,1024,512]{2,1,0:T(8,128)S(1)} %bitcast_dynamic-update-slice_fusion.1) | copy-start | bytes 50331652
Sparse Core Ops, SparseCore 0:
  85.1 90.1 all-gather.2
  213.8 62.5 all-reduce.3
